TPU v7x, 32 devices: a whole 2x2x4 slice. The times are simulated.
32 devices in a mesh: fsdp: 4 (over y, core), ctx: 8 (over z, x).
Axes of the slice: x: 2, y: 2, z: 4, core: 2. Of those that a mesh axis runs over, the one named last changes fastest.
Arguments:
- stream_in: bfloat16 [8192, 767], P(('fsdp', 'ctx')), as said below
- gain_attn: bfloat16 [768], P('fsdp'), may hold values from 0.5 to 1.5
- w_qkv: bfloat16 [768, 2304], P('fsdp'), may hold values from -0.3125 to 0.3125
- bias_qv: bfloat16 [1536], P('fsdp'), may hold values from -4 to 4
- w_out: bfloat16 [768, 768], P('fsdp'), may hold values from -2 to 2
- bias_out: bfloat16 [768], P('fsdp'), may hold values from -4 to 4
- gain_mlp: bfloat16 [768], P('fsdp'), may hold values from 0.5 to 1.5
- w_up: bfloat16 [768, 3072], P('fsdp'), may hold values from -0.21875 to 0.21875
- bias_up: bfloat16 [3072], P('fsdp'), may hold values from -4 to 4
- w_down: bfloat16 [3072, 768], P('fsdp'), may hold values from -0.109375 to 0.109375
- bias_down: bfloat16 [768], P('fsdp'), may hold values from -4 to 4
- grad_out: bfloat16 [8192, 767], P(('fsdp', 'ctx')), may hold values from -6 to 6
Outputs:
- stream_out: bfloat16 [8192, 767], P(('fsdp', 'ctx'))
- grad_stream: float32 [8192, 767], P(('fsdp', 'ctx'))
- grad_gain_attn: float32 [768], P('fsdp')
- grad_w_qkv: float32 [768, 2304], P('fsdp')
- grad_bias_qv: float32 [1536], P('fsdp')
- grad_w_out: float32 [768, 768], P('fsdp')
- grad_bias_out: float32 [768], P('fsdp')
- grad_gain_mlp: float32 [768], P('fsdp')
- grad_w_up: float32 [768, 3072], P('fsdp')
- grad_bias_up: float32 [3072], P('fsdp')
- grad_w_down: float32 [3072, 768], P('fsdp')
- grad_bias_down: float32 [768], P('fsdp')
Inputs may be any that keep to these rules, and one draw needn't show every extreme that they name: `stream_in`: every row is the first 767 entries of a zero-mean row of 768 entries, given as differences of neighbouring entries of a random row.
All inputs are finite; a program needn't handle non-finite values.
Results may differ from a plain program's by a relative error of at most 0.018.
Values may be sent and summed in bfloat16 or wider, within the bound.
No kernel may reach another device: no remote copies, remote signals or barrier semaphores. Data moves between devices by JAX's collectives and lax.ppermute only.
A program may use at most 192 MiB of HBM per device.

v0:
```python
import jax
import jax.numpy as jnp
from jax import lax
from jax.sharding import PartitionSpec as P

D = 768
H = 12
HD = 64
BLOCK = 256


norm_eps = 1e-05
neg_big = -1e30
block_rows = 512


def from_behind(value, axis, steps):
    count = lax.axis_size(axis)
    pairs = [(source, (source + steps) % count) for source in range(count)]
    return lax.ppermute(value, axis, pairs)


def scaled_norm(stream, gain_vec):
    return (
        stream * lax.rsqrt(jnp.mean(stream * stream, axis=1, keepdims=True) + norm_eps) * gain_vec
    )


def centered(branch):
    return branch - jnp.mean(branch, axis=1, keepdims=True)


def gelu_tanh(hidden):
    return jax.nn.gelu(hidden, approximate=True)


def visible(query_pos, key_pos):
    return key_pos[None, :] // BLOCK <= query_pos[:, None] // BLOCK


def split_heads(matrix):
    return matrix.reshape(matrix.shape[0], H, matrix.shape[1] // H)


def over_blocks(step_fn, carried, pieces):
    row_total = pieces[0].shape[0]
    block_count = row_total // block_rows
    stacked = tuple(
        (
            shard_piece.reshape((block_count, block_rows) + shard_piece.shape[1:])
            for shard_piece in pieces
        )
    )
    offsets = jnp.arange(block_count, dtype=jnp.int32) * block_rows

    def one_block(current, inputs):
        return (step_fn(current, inputs[:-1], inputs[-1]), None)

    ending, unused_out = lax.scan(one_block, carried, stacked + (offsets,))
    return ending


def forward_piece(carried, key_block, value_block, key_start, query_heads, query_pos):
    maxima, totals, accumulated = carried
    key_pos = key_start + jnp.arange(key_block.shape[0], dtype=jnp.int32)
    allowed = visible(query_pos, key_pos)[None]
    scores = jnp.einsum("qhd,khd->hqk", query_heads, key_block, preferred_element_type=jnp.float32)
    scores = jnp.where(allowed, scores, neg_big)
    new_max = jnp.maximum(maxima, jnp.max(scores, axis=2))
    weights = jnp.where(allowed, jnp.exp(scores - new_max[:, :, None]), 0.0)
    fading = jnp.exp(maxima - new_max)
    totals = totals * fading + jnp.sum(weights, axis=2)
    weights_low = weights.astype(jnp.bfloat16)
    accumulated = accumulated * fading[:, :, None] + jnp.einsum(
        "hqk,khd->hqd", weights_low, value_block, preferred_element_type=jnp.float32
    )
    return (new_max, totals, accumulated)


def backward_piece(
    key_block, value_block, key_pos, query_heads, grad_heads, log_sums, deltas, query_pos
):
    allowed = visible(query_pos, key_pos)[None]
    scores = jnp.einsum("qhd,khd->hqk", query_heads, key_block, preferred_element_type=jnp.float32)
    scores = jnp.where(allowed, scores, neg_big)
    chances = jnp.where(allowed, jnp.exp(scores - log_sums[:, :, None]), 0.0)
    grad_chances = jnp.einsum(
        "qhd,khd->hqk", grad_heads, value_block, preferred_element_type=jnp.float32
    )
    grad_scores = (chances * (grad_chances - deltas[:, :, None])).astype(jnp.bfloat16)
    query_grad = jnp.einsum(
        "hqk,khd->qhd", grad_scores, key_block, preferred_element_type=jnp.float32
    )
    key_grad = jnp.einsum(
        "hqk,qhd->khd", grad_scores, query_heads, preferred_element_type=jnp.float32
    )
    value_grad = jnp.einsum(
        "hqk,qhd->khd", chances.astype(jnp.bfloat16), grad_heads, preferred_element_type=jnp.float32
    )
    return (query_grad, key_grad, value_grad)


def local(
    stream_in,
    gain_attn,
    w_qkv,
    bias_qv,
    w_out,
    bias_out,
    gain_mlp,
    w_up,
    bias_up,
    w_down,
    bias_down,
    grad_out,
):
    tok_rows = stream_in.shape[0]
    gathered = (
        lax.all_gather(gain_attn, "fsdp", axis=0, tiled=True),
        lax.all_gather(w_qkv, "fsdp", axis=0, tiled=True),
        lax.all_gather(bias_qv, "fsdp", axis=0, tiled=True),
        lax.all_gather(w_out, "fsdp", axis=0, tiled=True),
        lax.all_gather(bias_out, "fsdp", axis=0, tiled=True),
        lax.all_gather(gain_mlp, "fsdp", axis=0, tiled=True),
        lax.all_gather(w_up, "fsdp", axis=0, tiled=True),
        lax.all_gather(bias_up, "fsdp", axis=0, tiled=True),
        lax.all_gather(w_down, "fsdp", axis=0, tiled=True),
        lax.all_gather(bias_down, "fsdp", axis=0, tiled=True),
    )
    (
        full_gain_attn,
        full_qkv,
        full_bias_qv,
        full_out,
        full_bias_out,
        full_gain_mlp,
        full_up,
        full_bias_up,
        full_down,
        full_bias_down,
    ) = gathered
    stream = stream_in.astype(jnp.float32)
    residual = jnp.concatenate([stream, -jnp.sum(stream, axis=1, keepdims=True)], axis=1)
    normed, norm_attn_back = jax.vjp(scaled_norm, residual, full_gain_attn.astype(jnp.float32))
    normed_low = normed.astype(jnp.bfloat16)
    bias_joined = jnp.concatenate(
        [full_bias_qv[:D], jnp.zeros((D,), jnp.bfloat16), full_bias_qv[D:]]
    ).astype(jnp.float32)
    joined_rows = jnp.dot(normed_low, full_qkv, preferred_element_type=jnp.float32) + bias_joined
    head_scale = HD ** (-0.5)
    queries = (joined_rows[:, :D] * head_scale).astype(jnp.bfloat16)
    key_rows = joined_rows[:, D : 2 * D].astype(jnp.bfloat16)
    values = joined_rows[:, 2 * D :].astype(jnp.bfloat16)
    ctx_index = lax.axis_index("ctx")
    query_pos = ctx_index * tok_rows + jnp.arange(tok_rows, dtype=jnp.int32)
    query_heads = split_heads(queries)
    last_block = query_pos[-1] // BLOCK

    def attend_step(carried, blocks, key_start):
        key_block = split_heads(blocks[0])
        value_block = split_heads(blocks[1])
        is_live = key_start // BLOCK <= last_block
        return lax.cond(
            is_live,
            lambda: forward_piece(
                carried, key_block, value_block, key_start, query_heads, query_pos
            ),
            lambda: carried,
        )

    start_state = (
        jnp.full((H, tok_rows), neg_big, jnp.float32),
        jnp.zeros((H, tok_rows), jnp.float32),
        jnp.zeros((H, tok_rows, HD), jnp.float32),
    )
    maxima, totals, accumulated = over_blocks(
        attend_step,
        start_state,
        (
            lax.all_gather(key_rows, "ctx", axis=0, tiled=True),
            lax.all_gather(values, "ctx", axis=0, tiled=True),
        ),
    )
    out_heads = accumulated / totals[:, :, None]
    log_sums = maxima + jnp.log(totals)
    attended = jnp.transpose(out_heads, (1, 0, 2)).reshape(tok_rows, D)
    attended_low = attended.astype(jnp.bfloat16)
    branch = jnp.dot(
        attended_low, full_out, preferred_element_type=jnp.float32
    ) + full_bias_out.astype(jnp.float32)
    middle = residual + centered(branch)
    normed_mlp, norm_mlp_back = jax.vjp(scaled_norm, middle, full_gain_mlp.astype(jnp.float32))
    normed_mlp_low = normed_mlp.astype(jnp.bfloat16)
    hidden = jnp.dot(
        normed_mlp_low, full_up, preferred_element_type=jnp.float32
    ) + full_bias_up.astype(jnp.float32)
    active, gelu_back = jax.vjp(gelu_tanh, hidden)
    active_low = active.astype(jnp.bfloat16)
    branch_mlp = jnp.dot(
        active_low, full_down, preferred_element_type=jnp.float32
    ) + full_bias_down.astype(jnp.float32)
    result = middle + centered(branch_mlp)
    stream_out = result[:, : D - 1].astype(jnp.bfloat16)
    back_qkv, back_out, back_up, back_down = (full_qkv, full_out, full_up, full_down)
    grad_result = jnp.concatenate(
        [grad_out.astype(jnp.float32), jnp.zeros((tok_rows, 1), jnp.float32)], axis=1
    )
    grad_branch_mlp = centered(grad_result).astype(jnp.bfloat16)
    part_down = jnp.einsum(
        "tf,td->fd", active_low, grad_branch_mlp, preferred_element_type=jnp.float32
    )
    part_bias_down = jnp.sum(grad_branch_mlp, axis=0, dtype=jnp.float32)
    grad_active = jnp.einsum(
        "td,fd->tf", grad_branch_mlp, back_down, preferred_element_type=jnp.float32
    )
    grad_hidden = gelu_back(grad_active)[0].astype(jnp.bfloat16)
    part_up = jnp.einsum(
        "td,tf->df", normed_mlp_low, grad_hidden, preferred_element_type=jnp.float32
    )
    part_bias_up = jnp.sum(grad_hidden, axis=0, dtype=jnp.float32)
    grad_normed_mlp = jnp.einsum(
        "tf,df->td", grad_hidden, back_up, preferred_element_type=jnp.float32
    )
    grad_middle_norm, part_gain_mlp = norm_mlp_back(grad_normed_mlp)
    grad_middle = grad_result + grad_middle_norm
    grad_branch = centered(grad_middle).astype(jnp.bfloat16)
    part_out = jnp.einsum(
        "te,td->ed", attended_low, grad_branch, preferred_element_type=jnp.float32
    )
    part_bias_out = jnp.sum(grad_branch, axis=0, dtype=jnp.float32)
    grad_attended = jnp.einsum(
        "td,ed->te", grad_branch, back_out, preferred_element_type=jnp.float32
    ).astype(jnp.bfloat16)
    grad_heads = split_heads(grad_attended)
    deltas = jnp.einsum("qhd,hqd->hq", grad_heads.astype(jnp.float32), out_heads)
    zero_heads = jnp.zeros((tok_rows, H, HD), jnp.float32)
    ctx_count = lax.axis_size("ctx")

    def cycle_step(cycle_turn, carried):
        key_now, value_now, key_acc, value_acc, query_acc = carried
        source = (ctx_index - cycle_turn) % ctx_count
        key_start = source * tok_rows
        key_pos = key_start + jnp.arange(tok_rows, dtype=jnp.int32)
        is_live = key_start // BLOCK <= last_block

        def compute():
            return backward_piece(
                split_heads(key_now.astype(jnp.bfloat16)),
                split_heads(value_now.astype(jnp.bfloat16)),
                key_pos,
                query_heads,
                grad_heads,
                log_sums,
                deltas,
                query_pos,
            )

        def skipped():
            return (zero_heads, zero_heads, zero_heads)

        query_add, key_add, value_add = lax.cond(is_live, compute, skipped)
        key_now, value_now, key_acc, value_acc = (
            from_behind(key_now.astype(jnp.bfloat16), "ctx", 1).astype(key_now.dtype),
            from_behind(value_now.astype(jnp.bfloat16), "ctx", 1).astype(value_now.dtype),
            from_behind((key_acc + key_add).astype(jnp.bfloat16), "ctx", 1).astype(jnp.float32),
            from_behind((value_acc + value_add).astype(jnp.bfloat16), "ctx", 1).astype(jnp.float32),
        )
        return (key_now, value_now, key_acc, value_acc, query_acc + query_add)

    cycle_start = (
        key_rows.astype(jnp.float32),
        values.astype(jnp.float32),
        zero_heads,
        zero_heads,
        zero_heads,
    )
    cycle_final = lax.fori_loop(0, ctx_count, cycle_step, cycle_start)
    query_grad = cycle_final[4]
    key_grad = cycle_final[2]
    value_grad = cycle_final[3]
    grad_joined = jnp.concatenate(
        [
            query_grad.reshape(tok_rows, D) * head_scale,
            key_grad.reshape(tok_rows, D),
            value_grad.reshape(tok_rows, D),
        ],
        axis=1,
    ).astype(jnp.bfloat16)
    part_qkv = jnp.einsum("td,te->de", normed_low, grad_joined, preferred_element_type=jnp.float32)
    part_bias_qv = jnp.concatenate(
        [
            jnp.sum(grad_joined[:, :D], axis=0, dtype=jnp.float32),
            jnp.sum(grad_joined[:, 2 * D :], axis=0, dtype=jnp.float32),
        ]
    )
    grad_normed = jnp.einsum("te,de->td", grad_joined, back_qkv, preferred_element_type=jnp.float32)
    grad_resid_norm, part_gain_attn = norm_attn_back(grad_normed)
    grad_resid = grad_middle + grad_resid_norm
    grad_stream = grad_resid[:, : D - 1] - grad_resid[:, D - 1 :]
    partials = (
        part_gain_attn,
        part_qkv,
        part_bias_qv,
        part_out,
        part_bias_out,
        part_gain_mlp,
        part_up,
        part_bias_up,
        part_down,
        part_bias_down,
    )
    shares = (
        lax.psum_scatter(
            partials[0].astype(jnp.bfloat16), "fsdp", scatter_dimension=0, tiled=True
        ).astype(jnp.float32),
        lax.psum_scatter(
            partials[1].astype(jnp.bfloat16), "fsdp", scatter_dimension=0, tiled=True
        ).astype(jnp.float32),
        lax.psum_scatter(
            partials[2].astype(jnp.bfloat16), "fsdp", scatter_dimension=0, tiled=True
        ).astype(jnp.float32),
        lax.psum_scatter(
            partials[3].astype(jnp.bfloat16), "fsdp", scatter_dimension=0, tiled=True
        ).astype(jnp.float32),
        lax.psum_scatter(
            partials[4].astype(jnp.bfloat16), "fsdp", scatter_dimension=0, tiled=True
        ).astype(jnp.float32),
        lax.psum_scatter(
            partials[5].astype(jnp.bfloat16), "fsdp", scatter_dimension=0, tiled=True
        ).astype(jnp.float32),
        lax.psum_scatter(
            partials[6].astype(jnp.bfloat16), "fsdp", scatter_dimension=0, tiled=True
        ).astype(jnp.float32),
        lax.psum_scatter(
            partials[7].astype(jnp.bfloat16), "fsdp", scatter_dimension=0, tiled=True
        ).astype(jnp.float32),
        lax.psum_scatter(
            partials[8].astype(jnp.bfloat16), "fsdp", scatter_dimension=0, tiled=True
        ).astype(jnp.float32),
        lax.psum_scatter(
            partials[9].astype(jnp.bfloat16), "fsdp", scatter_dimension=0, tiled=True
        ).astype(jnp.float32),
    )
    summed = lax.psum(
        (
            shares[0],
            shares[1],
            shares[2],
            shares[3],
            shares[4],
            shares[5],
            shares[6],
            shares[7],
            shares[8],
            shares[9],
        ),
        "ctx",
    )
    return (
        stream_out,
        grad_stream,
        summed[0],
        summed[1],
        summed[2],
        summed[3],
        summed[4],
        summed[5],
        summed[6],
        summed[7],
        summed[8],
        summed[9],
    )


def solution(mesh):
    return jax.shard_map(
        local,
        mesh=mesh,
        in_specs=(
            P(("fsdp", "ctx"), None),
            P("fsdp"),
            P("fsdp", None),
            P("fsdp"),
            P("fsdp", None),
            P("fsdp"),
            P("fsdp"),
            P("fsdp", None),
            P("fsdp"),
            P("fsdp", None),
            P("fsdp"),
            P(("fsdp", "ctx"), None),
        ),
        out_specs=(
            P(("fsdp", "ctx"), None),
            P(("fsdp", "ctx"), None),
            P("fsdp"),
            P("fsdp", None),
            P("fsdp"),
            P("fsdp", None),
            P("fsdp"),
            P("fsdp"),
            P("fsdp", None),
            P("fsdp"),
            P("fsdp", None),
            P("fsdp"),
        ),
        check_vma=False,
    )
```

profile of v0, /device:TPU:0, one launch (start us, length us, event | category | flops | bytes accessed | tf_op | source)
XLA Modules:
  0.0 1062.4 jit_solution(5491417915812893605)
XLA Ops:
  19.4 8.3 all-reduce.13
  30.7 12.7 %all-gather.9.cloned.1.call-done = bf16[768,2304]{1,0:T(8,128)(2,1)} async-done(((bf16[192,2304]{1,0:T(8,128)(2,1)}), bf16[768,2304]{1,0:T(8,128)(2,1)}) %all-gather.9.cloned.1.call-update) | async-done | bytes 3538960 | tf_op jit(solution)/shard_map/all_gather | solution.py:120
  65.8 42.3 %all-gather.11.cloned.1.call-done = bf16[2048,768]{1,0:T(8,128)(2,1)} async-done(((bf16[256,768]{1,0:T(8,128)(2,1)}), bf16[2048,768]{1,0:T(8,128)(2,1)}) %all-gather.11.cloned.1.call-update) | async-done | bytes 3145744 | tf_op jit(solution)/shard_map/all_gather | solution.py:180
  112.7 57.2 %all-gather.13.cloned.1.call-done = bf16[2048,768]{1,0:T(8,128)(2,1)} async-done(((bf16[256,768]{1,0:T(8,128)(2,1)}), bf16[2048,768]{1,0:T(8,128)(2,1)}) %all-gather.13.cloned.1.call-update) | async-done | bytes 3145744 | tf_op jit(solution)/shard_map/all_gather | solution.py:181
  174.8 19.3 %while.41 = (s32[]{:T(128)}, f32[12,256]{1,0:T(8,128)S(1)}, f32[12,256]{1,0:T(8,128)S(1)}, f32[12,256,64]{1,2,0:T(8,128)S(1)}, s32[4]{0:T(128)S(1)}, /*index=5*/...) while((s32[]{:T(128)}, f32[12,256]{1,0:T(8,128)S(1)}, ...), condition=%wide.region_7.8_spmd.clone, body=%wide.region_2.7_spmd.clone.sunk | while | flops 418924576 | bytes 26288600 | solution.py:59
  199.5 26.9 %all-gather.17.cloned.1.call-done = bf16[768,3072]{1,0:T(8,128)(2,1)} async-done(((bf16[192,3072]{1,0:T(8,128)(2,1)}), bf16[768,3072]{1,0:T(8,128)(2,1)}) %all-gather.17.cloned.1.call-update) | async-done | bytes 4718608 | tf_op jit(solution)/shard_map/all_gather | solution.py:125
  231.9 33.4 %all-gather.19.cloned.1.call-done = bf16[3072,768]{1,0:T(8,128)(2,1)} async-done(((bf16[768,768]{1,0:T(8,128)(2,1)}), bf16[3072,768]{1,0:T(8,128)(2,1)}) %all-gather.19.cloned.1.call-update) | async-done | bytes 4718608 | tf_op jit(solution)/shard_map/all_gather | solution.py:127
  265.3 7.5 fusion.64
  282.9 346.8 %while.42 = (s32[]{:T(128)}, bf16[256,768]{0,1:T(8,128)(2,1)S(1)}, bf16[256,768]{0,1:T(8,128)(2,1)S(1)}, f32[256,12,64]{0,2,1:T(8,128)}, f32[256,12,64]{0,2,1:T(...) while((s32[]{:T(128)}, bf16[256,768]{0,1:T(8,128)(2,1)S(1)}, ...), condition=%wide.region_17.18_spmd.clone, body=%wide.region_14.17_spmd.clone.sunk | while | flops 513220640 | bytes 36122412 | solution.py:277
  298.1 7.8 collective-permute-done.2
  306.9 7.4 collective-permute-done.3
  315.3 7.4 collective-permute-done
  322.7 7.8 collective-permute-done.1
  352.2 7.4 collective-permute-done.3
  379.5 8.2 collective-permute-start.3
  397.2 7.4 collective-permute-done.3
  405.6 7.4 collective-permute-done
  441.8 7.4 collective-permute-done.3
  450.2 7.4 collective-permute-done
  470.3 9.2 collective-permute-start.1
  485.7 7.4 collective-permute-done.3
  494.2 7.4 collective-permute-done
  518.7 9.0 collective-permute-done.2
  528.8 7.4 collective-permute-done.3
  557.2 12.6 %collective-permute-done.2 = bf16[256,12,64]{0,2,1:T(8,128)(2,1)S(1)} collective-permute-done((bf16[256,12,64]{0,2,1:T(8,128)(2,1)}, bf16[256,12,64]{0,2,1:T(8,128)(2,1)S(1)}, u32[]{:S(2)}, u32[]{:S(2)}) %collective-permute-start.2) | collective-permute-done | bytes 393248 | tf_op jit(solution)/shard_map/while/body/eval_jaxpr/ppermute | solution.py:20
  570.9 7.4 collective-permute-done.3
  596.0 15.0 %collective-permute-done.2 = bf16[256,12,64]{0,2,1:T(8,128)(2,1)S(1)} collective-permute-done((bf16[256,12,64]{0,2,1:T(8,128)(2,1)}, bf16[256,12,64]{0,2,1:T(8,128)(2,1)S(1)}, u32[]{:S(2)}, u32[]{:S(2)}) %collective-permute-start.2) | collective-permute-done | bytes 393248 | tf_op jit(solution)/shard_map/while/body/eval_jaxpr/ppermute | solution.py:20
  612.0 7.4 collective-permute-done.3
  657.2 11.9 %all-reduce.12 = (bf16[768]{0:T(1024)(128)(2,1)S(1)}, bf16[768]{0:T(1024)(128)(2,1)S(1)}, bf16[1536]{0:T(1024)(128)(2,1)S(1)}, bf16[768]{0:T(1024)(128)(2,1)S(1)...) all-reduce(bf16[768]{0:T(1024)(128)(2,1)S(1)} %dynamic-update-slice, ...), channel_id=1, replica_groups=mesh['fsdp'=4,'ctx'=8] {'fsdp'}, use_global_device_ids=true, to_apply=%add.4 | all-reduce | flops 8448 | bytes 33792
  677.3 48.8 %reduce-scatter.9.cloned.1.call-done = bf16[192,3072]{1,0:T(8,128)(2,1)} async-done(((bf16[768,3072]{1,0:T(8,128)(2,1)}), bf16[192,3072]{1,0:T(8,128)(2,1)}) %reduce-scatter.9.cloned.1.call-update) | async-done | bytes 1179664 | tf_op jit(solution)/shard_map/reduce_scatter | solution.py:331
  726.1 50.4 %reduce-scatter.11.cloned.1.call-done = bf16[768,768]{1,0:T(8,128)(2,1)} async-done(((bf16[3072,768]{1,0:T(8,128)(2,1)}), bf16[768,768]{1,0:T(8,128)(2,1)}) %reduce-scatter.11.cloned.1.call-update) | async-done | bytes 1179664 | tf_op jit(solution)/shard_map/reduce_scatter | solution.py:337
  776.5 279.0 %all-reduce.15 = (f32[192]{0:T(256)}, f32[192,2304]{1,0:T(8,128)}, f32[384]{0:T(512)}, f32[192,768]{1,0:T(8,128)}, f32[192]{0:T(256)}, /*index=5*/f32[192]{0:T(2...) all-reduce(f32[192]{0:T(256)S(1)} %dynamic-slice_convert_fusion.5, ...), channel_id=1, replica_groups=mesh['fsdp'=4,'ctx'=8] {'ctx'}, use_global_device_ids=true, to_apply=%region_21.22 | all-reduce | flops 1771392 | bytes 10632192 | tf_op jit(solution)/shard_map/psum | solution.py:344
  (367 shorter events, 308.1 us)
Async XLA Ops:
  7.2 36.2 %all-gather.9.cloned.1.call-start = ((), (), s32[]{:S(2)}) async-start(), calls=%async_computation.4 | async-start | bytes 4423680 | tf_op jit(solution)/shard_map/all_gather | solution.py:120
  7.9 100.2 %all-gather.11.cloned.1.call-start = ((), (), s32[]{:S(2)}) async-start(), calls=%async_computation.5 | async-start | bytes 3538944 | tf_op jit(solution)/shard_map/all_gather | solution.py:180
  47.5 122.4 %all-gather.13.cloned.1.call-start = ((), (), s32[]{:S(2)}) async-start(), calls=%async_computation.6 | async-start | bytes 3538944 | tf_op jit(solution)/shard_map/all_gather | solution.py:181
  48.2 146.0 %all-gather.15.cloned.1.call-start = ((), (), s32[]{:S(2)}) async-start(), calls=%async_computation.7 | async-start | bytes 1474560 | tf_op jit(solution)/shard_map/all_gather | solution.py:122
  48.8 177.6 %all-gather.17.cloned.1.call-start = ((), (), s32[]{:S(2)}) async-start(), calls=%async_computation.8 | async-start | bytes 5898240 | tf_op jit(solution)/shard_map/all_gather | solution.py:125
  49.4 215.9 %all-gather.19.cloned.1.call-start = ((), (), s32[]{:S(2)}) async-start(), calls=%async_computation.9 | async-start | bytes 5898240 | tf_op jit(solution)/shard_map/all_gather | solution.py:127
  50.0 627.3 %reduce-scatter.7.cloned.1.call-start = ((), (), s32[]{:S(2)}) async-start(), calls=%async_computation.11 | async-start | bytes 1474560 | tf_op jit(solution)/shard_map/reduce_scatter | solution.py:322
  282.9 394.4 %reduce-scatter.5.cloned.1.call-start = ((), (), s32[]{:S(2)}) async-start(), calls=%async_computation.10 | async-start | bytes 4423680 | tf_op jit(solution)/shard_map/reduce_scatter | solution.py:316
  294.2 28.6 %collective-permute-start = (bf16[256,768]{0,1:T(8,128)(2,1)S(1)}, bf16[256,768]{0,1:T(8,128)(2,1)S(1)}, u32[]{:S(2)}, u32[]{:S(2)}) collective-permute-start(bf16[256,768]{0,1:T(8,128)(2,1)S(1)} %copy.92), channel_id=1, source_target_pairs={{0,1},{1,2},{2,3},{3,4},{4,5},{5,6},{6,7},{7,0},{8,9},{9,10},{10,1... | collective-permute-start | bytes 1179656 | tf_op jit(solution)/shard_map/while/body/eval_jaxpr/ppermute | solution.py:20
  295.6 34.8 %collective-permute-start.1 = (bf16[256,768]{0,1:T(8,128)(2,1)}, bf16[256,768]{0,1:T(8,128)(2,1)S(1)}, u32[]{:S(2)}, u32[]{:S(2)}) collective-permute-start(bf16[256,768]{0,1:T(8,128)(2,1)} %copy.93), channel_id=1, source_target_pairs={{0,1},{1,2},{2,3},{3,4},{4,5},{5,6},{6,7},{7,0},{8,9},{9,10},{10,1... | collective-permute-start | bytes 1179656 | tf_op jit(solution)/shard_map/while/body/eval_jaxpr/ppermute | solution.py:20
  341.9 26.1 %collective-permute-start = (bf16[256,768]{0,1:T(8,128)(2,1)S(1)}, bf16[256,768]{0,1:T(8,128)(2,1)S(1)}, u32[]{:S(2)}, u32[]{:S(2)}) collective-permute-start(bf16[256,768]{0,1:T(8,128)(2,1)S(1)} %copy.92), channel_id=1, source_target_pairs={{0,1},{1,2},{2,3},{3,4},{4,5},{5,6},{6,7},{7,0},{8,9},{9,10},{10,1... | collective-permute-start | bytes 1179656 | tf_op jit(solution)/shard_map/while/body/eval_jaxpr/ppermute | solution.py:20
  342.5 32.7 %collective-permute-start.1 = (bf16[256,768]{0,1:T(8,128)(2,1)}, bf16[256,768]{0,1:T(8,128)(2,1)S(1)}, u32[]{:S(2)}, u32[]{:S(2)}) collective-permute-start(bf16[256,768]{0,1:T(8,128)(2,1)} %copy.93), channel_id=1, source_target_pairs={{0,1},{1,2},{2,3},{3,4},{4,5},{5,6},{6,7},{7,0},{8,9},{9,10},{10,1... | collective-permute-start | bytes 1179656 | tf_op jit(solution)/shard_map/while/body/eval_jaxpr/ppermute | solution.py:20
  379.5 25.1 %collective-permute-start.3 = (bf16[256,12,64]{0,2,1:T(8,128)(2,1)S(1)}, bf16[256,12,64]{0,2,1:T(8,128)(2,1)S(1)}, u32[]{:S(2)}, u32[]{:S(2)}) collective-permute-start(bf16[256,12,64]{0,2,1:T(8,128)(2,1)S(1)} %fusion.96), channel_id=1, source_target_pairs={{0,1},{1,2},{2,3},{3,4},{4,5},{5,6},{6,7},{7,0},{8,9},{9,10},{10,1... | collective-permute-start | bytes 1179656 | tf_op jit(solution)/shard_map/while/body/eval_jaxpr/ppermute | solution.py:20
  387.7 25.3 %collective-permute-start = (bf16[256,768]{0,1:T(8,128)(2,1)S(1)}, bf16[256,768]{0,1:T(8,128)(2,1)S(1)}, u32[]{:S(2)}, u32[]{:S(2)}) collective-permute-start(bf16[256,768]{0,1:T(8,128)(2,1)S(1)} %copy.92), channel_id=1, source_target_pairs={{0,1},{1,2},{2,3},{3,4},{4,5},{5,6},{6,7},{7,0},{8,9},{9,10},{10,1... | collective-permute-start | bytes 1179656 | tf_op jit(solution)/shard_map/while/body/eval_jaxpr/ppermute | solution.py:20
  387.8 31.4 %collective-permute-start.1 = (bf16[256,768]{0,1:T(8,128)(2,1)}, bf16[256,768]{0,1:T(8,128)(2,1)S(1)}, u32[]{:S(2)}, u32[]{:S(2)}) collective-permute-start(bf16[256,768]{0,1:T(8,128)(2,1)} %copy.93), channel_id=1, source_target_pairs={{0,1},{1,2},{2,3},{3,4},{4,5},{5,6},{6,7},{7,0},{8,9},{9,10},{10,1... | collective-permute-start | bytes 1179656 | tf_op jit(solution)/shard_map/while/body/eval_jaxpr/ppermute | solution.py:20
  423.5 25.7 %collective-permute-start.3 = (bf16[256,12,64]{0,2,1:T(8,128)(2,1)S(1)}, bf16[256,12,64]{0,2,1:T(8,128)(2,1)S(1)}, u32[]{:S(2)}, u32[]{:S(2)}) collective-permute-start(bf16[256,12,64]{0,2,1:T(8,128)(2,1)S(1)} %fusion.96), channel_id=1, source_target_pairs={{0,1},{1,2},{2,3},{3,4},{4,5},{5,6},{6,7},{7,0},{8,9},{9,10},{10,1... | collective-permute-start | bytes 1179656 | tf_op jit(solution)/shard_map/while/body/eval_jaxpr/ppermute | solution.py:20
  426.6 30.9 %collective-permute-start = (bf16[256,768]{0,1:T(8,128)(2,1)S(1)}, bf16[256,768]{0,1:T(8,128)(2,1)S(1)}, u32[]{:S(2)}, u32[]{:S(2)}) collective-permute-start(bf16[256,768]{0,1:T(8,128)(2,1)S(1)} %copy.92), channel_id=1, source_target_pairs={{0,1},{1,2},{2,3},{3,4},{4,5},{5,6},{6,7},{7,0},{8,9},{9,10},{10,1... | collective-permute-start | bytes 1179656 | tf_op jit(solution)/shard_map/while/body/eval_jaxpr/ppermute | solution.py:20
  432.3 30.8 %collective-permute-start.1 = (bf16[256,768]{0,1:T(8,128)(2,1)}, bf16[256,768]{0,1:T(8,128)(2,1)S(1)}, u32[]{:S(2)}, u32[]{:S(2)}) collective-permute-start(bf16[256,768]{0,1:T(8,128)(2,1)} %copy.93), channel_id=1, source_target_pairs={{0,1},{1,2},{2,3},{3,4},{4,5},{5,6},{6,7},{7,0},{8,9},{9,10},{10,1... | collective-permute-start | bytes 1179656 | tf_op jit(solution)/shard_map/while/body/eval_jaxpr/ppermute | solution.py:20
  467.4 25.7 %collective-permute-start.3 = (bf16[256,12,64]{0,2,1:T(8,128)(2,1)S(1)}, bf16[256,12,64]{0,2,1:T(8,128)(2,1)S(1)}, u32[]{:S(2)}, u32[]{:S(2)}) collective-permute-start(bf16[256,12,64]{0,2,1:T(8,128)(2,1)S(1)} %fusion.96), channel_id=1, source_target_pairs={{0,1},{1,2},{2,3},{3,4},{4,5},{5,6},{6,7},{7,0},{8,9},{9,10},{10,1... | collective-permute-start | bytes 1179656 | tf_op jit(solution)/shard_map/while/body/eval_jaxpr/ppermute | solution.py:20
  467.5 34.1 %collective-permute-start = (bf16[256,768]{0,1:T(8,128)(2,1)S(1)}, bf16[256,768]{0,1:T(8,128)(2,1)S(1)}, u32[]{:S(2)}, u32[]{:S(2)}) collective-permute-start(bf16[256,768]{0,1:T(8,128)(2,1)S(1)} %copy.92), channel_id=1, source_target_pairs={{0,1},{1,2},{2,3},{3,4},{4,5},{5,6},{6,7},{7,0},{8,9},{9,10},{10,1... | collective-permute-start | bytes 1179656 | tf_op jit(solution)/shard_map/while/body/eval_jaxpr/ppermute | solution.py:20
  470.3 35.9 %collective-permute-start.1 = (bf16[256,768]{0,1:T(8,128)(2,1)}, bf16[256,768]{0,1:T(8,128)(2,1)S(1)}, u32[]{:S(2)}, u32[]{:S(2)}) collective-permute-start(bf16[256,768]{0,1:T(8,128)(2,1)} %copy.93), channel_id=1, source_target_pairs={{0,1},{1,2},{2,3},{3,4},{4,5},{5,6},{6,7},{7,0},{8,9},{9,10},{10,1... | collective-permute-start | bytes 1179656 | tf_op jit(solution)/shard_map/while/body/eval_jaxpr/ppermute | solution.py:20
  510.4 25.7 %collective-permute-start.3 = (bf16[256,12,64]{0,2,1:T(8,128)(2,1)S(1)}, bf16[256,12,64]{0,2,1:T(8,128)(2,1)S(1)}, u32[]{:S(2)}, u32[]{:S(2)}) collective-permute-start(bf16[256,12,64]{0,2,1:T(8,128)(2,1)S(1)} %fusion.96), channel_id=1, source_target_pairs={{0,1},{1,2},{2,3},{3,4},{4,5},{5,6},{6,7},{7,0},{8,9},{9,10},{10,1... | collective-permute-start | bytes 1179656 | tf_op jit(solution)/shard_map/while/body/eval_jaxpr/ppermute | solution.py:20
  510.5 33.5 %collective-permute-start = (bf16[256,768]{0,1:T(8,128)(2,1)S(1)}, bf16[256,768]{0,1:T(8,128)(2,1)S(1)}, u32[]{:S(2)}, u32[]{:S(2)}) collective-permute-start(bf16[256,768]{0,1:T(8,128)(2,1)S(1)} %copy.92), channel_id=1, source_target_pairs={{0,1},{1,2},{2,3},{3,4},{4,5},{5,6},{6,7},{7,0},{8,9},{9,10},{10,1... | collective-permute-start | bytes 1179656 | tf_op jit(solution)/shard_map/while/body/eval_jaxpr/ppermute | solution.py:20
  513.3 34.9 %collective-permute-start.1 = (bf16[256,768]{0,1:T(8,128)(2,1)}, bf16[256,768]{0,1:T(8,128)(2,1)S(1)}, u32[]{:S(2)}, u32[]{:S(2)}) collective-permute-start(bf16[256,768]{0,1:T(8,128)(2,1)} %copy.93), channel_id=1, source_target_pairs={{0,1},{1,2},{2,3},{3,4},{4,5},{5,6},{6,7},{7,0},{8,9},{9,10},{10,1... | collective-permute-start | bytes 1179656 | tf_op jit(solution)/shard_map/while/body/eval_jaxpr/ppermute | solution.py:20
  552.5 25.7 %collective-permute-start.3 = (bf16[256,12,64]{0,2,1:T(8,128)(2,1)S(1)}, bf16[256,12,64]{0,2,1:T(8,128)(2,1)S(1)}, u32[]{:S(2)}, u32[]{:S(2)}) collective-permute-start(bf16[256,12,64]{0,2,1:T(8,128)(2,1)S(1)} %fusion.96), channel_id=1, source_target_pairs={{0,1},{1,2},{2,3},{3,4},{4,5},{5,6},{6,7},{7,0},{8,9},{9,10},{10,1... | collective-permute-start | bytes 1179656 | tf_op jit(solution)/shard_map/while/body/eval_jaxpr/ppermute | solution.py:20
  552.6 32.6 %collective-permute-start = (bf16[256,768]{0,1:T(8,128)(2,1)S(1)}, bf16[256,768]{0,1:T(8,128)(2,1)S(1)}, u32[]{:S(2)}, u32[]{:S(2)}) collective-permute-start(bf16[256,768]{0,1:T(8,128)(2,1)S(1)} %copy.92), channel_id=1, source_target_pairs={{0,1},{1,2},{2,3},{3,4},{4,5},{5,6},{6,7},{7,0},{8,9},{9,10},{10,1... | collective-permute-start | bytes 1179656 | tf_op jit(solution)/shard_map/while/body/eval_jaxpr/ppermute | solution.py:20
  552.7 36.8 %collective-permute-start.1 = (bf16[256,768]{0,1:T(8,128)(2,1)}, bf16[256,768]{0,1:T(8,128)(2,1)S(1)}, u32[]{:S(2)}, u32[]{:S(2)}) collective-permute-start(bf16[256,768]{0,1:T(8,128)(2,1)} %copy.93), channel_id=1, source_target_pairs={{0,1},{1,2},{2,3},{3,4},{4,5},{5,6},{6,7},{7,0},{8,9},{9,10},{10,1... | collective-permute-start | bytes 1179656 | tf_op jit(solution)/shard_map/while/body/eval_jaxpr/ppermute | solution.py:20
  593.7 25.7 %collective-permute-start.3 = (bf16[256,12,64]{0,2,1:T(8,128)(2,1)S(1)}, bf16[256,12,64]{0,2,1:T(8,128)(2,1)S(1)}, u32[]{:S(2)}, u32[]{:S(2)}) collective-permute-start(bf16[256,12,64]{0,2,1:T(8,128)(2,1)S(1)} %fusion.96), channel_id=1, source_target_pairs={{0,1},{1,2},{2,3},{3,4},{4,5},{5,6},{6,7},{7,0},{8,9},{9,10},{10,1... | collective-permute-start | bytes 1179656 | tf_op jit(solution)/shard_map/while/body/eval_jaxpr/ppermute | solution.py:20
  593.8 31.7 %collective-permute-start = (bf16[256,768]{0,1:T(8,128)(2,1)S(1)}, bf16[256,768]{0,1:T(8,128)(2,1)S(1)}, u32[]{:S(2)}, u32[]{:S(2)}) collective-permute-start(bf16[256,768]{0,1:T(8,128)(2,1)S(1)} %copy.92), channel_id=1, source_target_pairs={{0,1},{1,2},{2,3},{3,4},{4,5},{5,6},{6,7},{7,0},{8,9},{9,10},{10,1... | collective-permute-start | bytes 1179656 | tf_op jit(solution)/shard_map/while/body/eval_jaxpr/ppermute | solution.py:20
  593.8 35.8 %collective-permute-start.1 = (bf16[256,768]{0,1:T(8,128)(2,1)}, bf16[256,768]{0,1:T(8,128)(2,1)S(1)}, u32[]{:S(2)}, u32[]{:S(2)}) collective-permute-start(bf16[256,768]{0,1:T(8,128)(2,1)} %copy.93), channel_id=1, source_target_pairs={{0,1},{1,2},{2,3},{3,4},{4,5},{5,6},{6,7},{7,0},{8,9},{9,10},{10,1... | collective-permute-start | bytes 1179656 | tf_op jit(solution)/shard_map/while/body/eval_jaxpr/ppermute | solution.py:20
  636.7 89.4 %reduce-scatter.9.cloned.1.call-start = ((), (), s32[]{:S(2)}) async-start(), calls=%async_computation.12 | async-start | bytes 5898240 | tf_op jit(solution)/shard_map/reduce_scatter | solution.py:331
  643.1 133.4 %reduce-scatter.11.cloned.1.call-start = ((), (), s32[]{:S(2)}) async-start(), calls=%async_computation.13 | async-start | bytes 5898240 | tf_op jit(solution)/shard_map/reduce_scatter | solution.py:337
  (55 other events, 833.7 us)
Sparse Core Ops, SparseCore 0:
  9.6 33.7 all-gather.8
  47.6 60.3 all-gather.10
  110.8 59.0 all-gather.12
  171.3 16.0 all-gather.14
  188.9 37.4 all-gather.16
  227.8 37.4 all-gather.18
  283.0 25.7 reduce-scatter.6
  636.9 38.7 reduce-scatter.4
  678.2 47.8 reduce-scatter.8
  728.6 47.8 reduce-scatter.10
where the time goes:
time: 1070 us; the launch traced here: 1060 us
  waiting for transfers between devices  491 us (46%)
  blocking collectives  310 us (29%)
  other arithmetic  77 us (7%)
  starting transfers between devices  60.7 us (6%)
  matrix products  55.2 us (5%)
  local copies, waits for them, and re-layouts  36.8 us (3%)
  between operations  20 us (2%)
  loops' own time  11.4 us (1%)
    psum x1, blocking collectives, local(): lax.psum((shares[0], shares[1], shares[2], shares[3], shares[4], shares[5...  279 us
    ppermute x32, waiting for transfers between devices, from_behind(): return lax.ppermute(value, axis, pairs)  216 us
    ppermute x32, starting transfers between devices, from_behind(): return lax.ppermute(value, axis, pairs)  60.3 us
    all_gather x1, waiting for transfers between devices, local(): lax.all_gather(values, 'ctx', axis=0, tiled=True)  57.2 us
    reduce_scatter x1, waiting for transfers between devices, local(): lax.psum_scatter(partials[8].astype(jnp.bfloat16), 'fsdp', scatter_dimens...  50.4 us
    reduce_scatter x1, waiting for transfers between devices, local(): lax.psum_scatter(partials[6].astype(jnp.bfloat16), 'fsdp', scatter_dimens...  48.8 us
    all_gather x1, waiting for transfers between devices, local(): lax.all_gather(key_rows, 'ctx', axis=0, tiled=True)  42.3 us
    all_gather x1, waiting for transfers between devices, local(): lax.all_gather(w_down, 'fsdp', axis=0, tiled=True)  33.4 us
  transfers between devices with their start and end apart: 42, of which 39 were waited for; matrix products, arithmetic and copies ran while one was open for 13% of the time, Pallas kernels for 0%

commit v1 on v0

v1 whole, which is shorter than its diff:
```python
import jax
import jax.numpy as jnp
from jax import lax
from jax.experimental import pallas as pl
from jax.experimental.pallas import tpu as pltpu
from jax.sharding import PartitionSpec as P

D = 768
H = 12
HD = 64
BLOCK = 256
HEAD_GROUPS = 4
GROUP_HEADS = H // HEAD_GROUPS
GROUP_COLS = GROUP_HEADS * HD
HEAD_SCALE = HD ** (-0.5)
NORM_EPS = 1e-05
NEG_BIG = -1e30
AXES = ("fsdp", "ctx")
VMEM_LIMIT = 100 << 19

f32 = jnp.float32
bf16 = jnp.bfloat16


def dot(left, right):
    return jnp.dot(left, right, preferred_element_type=f32)


def dot_tn(left, right):
    return lax.dot_general(left, right, (((0,), (0,)), ((), ())), preferred_element_type=f32)


def dot_nt(left, right):
    return lax.dot_general(left, right, (((1,), (1,)), ((), ())), preferred_element_type=f32)


def pick(value, index, axis=0):
    return lax.dynamic_index_in_dim(value, index, axis, keepdims=False)


def in_order(own, other, bit):
    return jnp.where(bit == 0, jnp.stack([own, other]), jnp.stack([other, own]))


def centered(branch):
    return branch - jnp.mean(branch, axis=1, keepdims=True)


def inverse_rms(stream):
    return lax.rsqrt(jnp.mean(stream * stream, axis=1, keepdims=True) + NORM_EPS)


def head_masked(value, head):
    if head == GROUP_HEADS - 1 and GROUP_HEADS % 2 == 1:
        return value[:, head * HD :], head * HD, HD
    start = (head // 2) * 2 * HD
    lanes = value[:, start : start + 2 * HD]
    at = lax.broadcasted_iota(jnp.int32, lanes.shape, 1) // HD
    return jnp.where(at == head % 2, lanes, jnp.zeros_like(lanes)), start, 2 * HD


def forward_kernel(member_ref, q_ref, k_ref, vt_ref, out_ref, log_ref):
    blocks, query_rows, _ = q_ref.shape
    rows = k_ref.shape[1]
    member = member_ref[0]

    def one_query_block(block, _):
        queries = q_ref[block ^ member]
        masked = [head_masked(queries, head) for head in range(GROUP_HEADS)]

        def one_key_block(key_block, carried):
            slot = key_block ^ member
            at = pl.multiple_of(slot * rows, rows)
            kept = []
            for head in range(GROUP_HEADS):
                top, total, acc = carried[head]
                query, start, width = masked[head]
                scores = dot_nt(k_ref[slot, :, start : start + width], query)
                new_top = jnp.maximum(top, jnp.max(scores, axis=0, keepdims=True))
                weights = jnp.exp(scores - new_top)
                fading = jnp.exp(top - new_top)
                total = total * fading + jnp.sum(weights, axis=0, keepdims=True)
                values = vt_ref[head * HD : (head + 1) * HD, pl.ds(at, rows)]
                acc = acc * fading + dot(values, weights.astype(bf16))
                kept.append((new_top, total, acc))
            return tuple(kept)

        start_state = tuple(
            (
                jnp.full((1, query_rows), NEG_BIG, f32),
                jnp.zeros((1, query_rows), f32),
                jnp.zeros((HD, query_rows), f32),
            )
            for _ in range(GROUP_HEADS)
        )
        ended = lax.fori_loop(0, block + 1, one_key_block, start_state)
        heads = jnp.concatenate([acc / total for _, total, acc in ended], axis=0)
        out_ref[block] = heads.T.astype(bf16)
        for head, (top, total, _) in enumerate(ended):
            log_ref[block, head : head + 1, :] = top + jnp.log(total)
        return 0

    lax.fori_loop(0, blocks, one_query_block, 0)


def attention_forward(member, queries, key_rows, values_t):
    blocks, query_rows, cols = queries.shape
    rows = key_rows.shape[1]
    scores = GROUP_HEADS * query_rows * rows * blocks * (blocks + 1) // 2
    return pl.pallas_call(
        forward_kernel,
        out_shape=(
            jax.ShapeDtypeStruct((blocks, query_rows, cols), bf16),
            jax.ShapeDtypeStruct((blocks, 8, query_rows), f32),
        ),
        in_specs=[pl.BlockSpec(memory_space=pltpu.SMEM)] + [pl.BlockSpec(memory_space=pltpu.VMEM)] * 3,
        out_specs=(pl.BlockSpec(memory_space=pltpu.VMEM),) * 2,
        compiler_params=pltpu.CompilerParams(vmem_limit_bytes=VMEM_LIMIT),
        cost_estimate=pl.CostEstimate(
            flops=4 * HD * scores, bytes_accessed=4 * rows * blocks * cols, transcendentals=scores
        ),
        name="attend",
    )(member, queries, key_rows, values_t)


def backward_kernel(
    member_ref, q_ref, k_ref, v_ref, kt_ref, g_ref, out_ref, log_ref, dq_ref, dk_ref, dv_ref, dk_acc, dv_acc, dq_acc, delta_ref
):
    blocks = q_ref.shape[0]
    rows = k_ref.shape[1]
    member = member_ref[0]

    def prepare(block, _):
        products = (g_ref[block].astype(f32) * out_ref[block].astype(f32)).T
        for head in range(GROUP_HEADS):
            part = products[head * HD : (head + 1) * HD]
            delta_ref[block, head : head + 1, :] = jnp.sum(part, axis=0, keepdims=True)
        return 0

    lax.fori_loop(0, blocks, prepare, 0)
    dq_acc[...] = jnp.zeros_like(dq_acc)

    def one_key_block(key_block, _):
        slot = key_block ^ member
        at = pl.multiple_of(slot * rows, rows)
        dk_acc[...] = jnp.zeros_like(dk_acc)
        dv_acc[...] = jnp.zeros_like(dv_acc)

        def one_query_block(block, _):
            queries, grads = q_ref[block ^ member], g_ref[block]
            for head in range(GROUP_HEADS):
                query, start, width = head_masked(queries, head)
                grad, _, _ = head_masked(grads, head)
                lanes = slice(start, start + width)
                scores = dot_nt(k_ref[slot, :, lanes], query)
                prob = jnp.exp(scores - log_ref[block, head : head + 1, :])
                grad_prob = dot_nt(v_ref[slot, :, lanes], grad)
                grad_scores = (prob * (grad_prob - delta_ref[block, head : head + 1, :])).astype(bf16)
                dv_acc[:, lanes] += dot(prob.astype(bf16), grad)
                dk_acc[:, lanes] += dot(grad_scores, query)
                part = slice(head * HD, (head + 1) * HD)
                dq_acc[block, part, :] += dot(kt_ref[part, pl.ds(at, rows)], grad_scores)
            return 0

        lax.fori_loop(key_block, blocks, one_query_block, 0)
        dk_ref[slot] = dk_acc[...].astype(bf16)
        dv_ref[slot] = dv_acc[...].astype(bf16)
        return 0

    lax.fori_loop(0, blocks, one_key_block, 0)

    def write(block, _):
        dq_ref[block ^ member] = (dq_acc[block].T * HEAD_SCALE).astype(bf16)
        return 0

    lax.fori_loop(0, blocks, write, 0)


def attention_backward(member, queries, key_rows, values, keys_t, grads, outs, logs):
    blocks, query_rows, cols = queries.shape
    rows = key_rows.shape[1]
    scores = GROUP_HEADS * query_rows * rows * blocks * (blocks + 1) // 2
    return pl.pallas_call(
        backward_kernel,
        out_shape=(
            jax.ShapeDtypeStruct((blocks, query_rows, cols), bf16),
            jax.ShapeDtypeStruct((blocks, rows, cols), bf16),
            jax.ShapeDtypeStruct((blocks, rows, cols), bf16),
        ),
        in_specs=[pl.BlockSpec(memory_space=pltpu.SMEM)] + [pl.BlockSpec(memory_space=pltpu.VMEM)] * 7,
        out_specs=(pl.BlockSpec(memory_space=pltpu.VMEM),) * 3,
        scratch_shapes=[
            pltpu.VMEM((rows, cols), f32),
            pltpu.VMEM((rows, cols), f32),
            pltpu.VMEM((blocks, cols, query_rows), f32),
            pltpu.VMEM((blocks, 8, query_rows), f32),
        ],
        compiler_params=pltpu.CompilerParams(vmem_limit_bytes=VMEM_LIMIT),
        cost_estimate=pl.CostEstimate(
            flops=10 * HD * scores, bytes_accessed=10 * rows * blocks * cols, transcendentals=scores
        ),
        name="attend_back",
    )(member, queries, key_rows, values, keys_t, grads, outs, logs)


def solution(mesh):
    fsdp_count, ctx_count = mesh.shape["fsdp"], mesh.shape["ctx"]
    half = ctx_count // 2
    steps = half.bit_length() - 1
    ctx_steps = steps + 1
    splits = ctx_count // HEAD_GROUPS
    shard = D // fsdp_count

    def send(value, target):
        pairs = []
        for source in range(fsdp_count * ctx_count):
            row, at = target(*divmod(source, ctx_count))
            pairs.append((source, row * ctx_count + at))
        return lax.ppermute(value, AXES, pairs)

    def to_core(value):
        return send(value, lambda row, at: (row ^ 1, at))

    def to_chip_row(value):
        return send(value, lambda row, at: (row ^ 2, at))

    def to_ctx(value, bit):
        return send(value, lambda row, at: (row, at ^ bit))

    def swap_sequences(value):
        return send(
            value, lambda row, at: (row, at) if (row & 1) == at // half else (row ^ 1, at ^ half)
        )

    groups = [
        [(row + core) * ctx_count + side * half + at for core in range(2) for at in range(half)]
        for row in range(0, fsdp_count, 2)
        for side in range(2)
    ]

    def group_all_to_all(value):
        return lax.all_to_all(value, AXES, 0, 0, axis_index_groups=groups, tiled=True)

    def reversed_bits(value):
        out = 0
        for at in range(steps):
            out = out | (((value >> at) & 1) << (steps - 1 - at))
        return out

    def local(
        stream_in,
        gain_attn,
        w_qkv,
        bias_qv,
        w_out,
        bias_out,
        gain_mlp,
        w_up,
        bias_up,
        w_down,
        bias_down,
        grad_out,
    ):
        rows = stream_in.shape[0]
        query_rows = rows // splits
        fsdp_at, ctx_at = lax.axis_index("fsdp"), lax.axis_index("ctx")
        core, chip_row = fsdp_at & 1, fsdp_at >> 1
        side, inner = ctx_at // half, ctx_at % half
        member = core * half + inner
        member_at = member.astype(jnp.int32).reshape(1)
        head_group = inner % HEAD_GROUPS
        query_split = member // HEAD_GROUPS

        def over_fsdp(value):
            pair = in_order(value, to_chip_row(value), chip_row)
            return jnp.swapaxes(in_order(pair, to_core(pair), core), 0, 1).reshape(
                (fsdp_count,) + value.shape
            )

        stream = swap_sequences(stream_in).astype(f32)
        grad_top = swap_sequences(grad_out).astype(f32)
        vectors = over_fsdp(
            jnp.concatenate([gain_attn, bias_qv, bias_out, gain_mlp, bias_up, bias_down])
        ).astype(f32)
        cuts, at = [], 0
        for part in (gain_attn, bias_qv, bias_out, gain_mlp, bias_up, bias_down):
            cuts.append(vectors[:, at : at + part.shape[0]])
            at += part.shape[0]
        gain_attn_all, bias_qv_all, bias_out_all, gain_mlp_all, _, bias_down_all = [
            cut.reshape(-1) for cut in cuts
        ]
        bias_up_half = pick(cuts[4].reshape(2, 2, -1), core, 1).reshape(-1)
        w_heads = over_fsdp(
            pick(w_qkv.reshape(shard, 3, HEAD_GROUPS, GROUP_COLS), head_group, 2).reshape(shard, -1)
        ).reshape(D, 3 * GROUP_COLS)
        w_out_all = over_fsdp(w_out).reshape(D, D)
        w_down_half = in_order(w_down, to_chip_row(w_down), chip_row).reshape(-1, D)
        up_parts = w_up.reshape(shard, 2, 2, -1)
        up_rows = in_order(pick(up_parts, core, 2), to_core(pick(up_parts, 1 - core, 2)), core)
        w_up_half = in_order(up_rows, to_chip_row(up_rows), chip_row).reshape(D, -1)

        resid = jnp.concatenate([stream, -jnp.sum(stream, axis=1, keepdims=True)], axis=1)
        inv_attn = inverse_rms(resid)
        unit = resid * inv_attn
        unit_low = unit.astype(bf16)
        first, second = unit_low[None, : rows // 2], unit_low[None, rows // 2 :]
        for step in range(steps):
            got = (to_ctx(first, 1 << step), to_ctx(second, 1 << (steps - 1 - step)))
            got = lax.optimization_barrier(got)
            first, second = jnp.concatenate([first, got[0]]), jnp.concatenate([second, got[1]])
        second = jnp.stack([second[reversed_bits(slot)] for slot in range(half)])
        both = jnp.concatenate([first, second], axis=1)
        gathered = jnp.concatenate([both, to_core(both)])
        normed = (gathered.astype(f32) * gain_attn_all).astype(bf16)
        normed_query = pick(normed.reshape(ctx_count, splits, query_rows, D), query_split, 1)

        wq, wk, wv = (w_heads[:, at * GROUP_COLS : (at + 1) * GROUP_COLS] for at in range(3))
        bias_parts = pick(bias_qv_all.reshape(2, HEAD_GROUPS, GROUP_COLS), head_group, 1)
        queries = ((dot(normed_query, wq) + bias_parts[0]) * HEAD_SCALE).astype(bf16)
        key_rows = dot(normed, wk).astype(bf16)
        values = (dot(normed, wv) + bias_parts[1]).astype(bf16)
        flat = normed.reshape(-1, D)
        keys_t = lax.dot_general(wk, flat, (((0,), (1,)), ((), ())), preferred_element_type=f32)
        values_t = lax.dot_general(wv, flat, (((0,), (1,)), ((), ())), preferred_element_type=f32)
        keys_t = keys_t.astype(bf16)
        values_t = (values_t + bias_parts[1][:, None]).astype(bf16)
        outs, logs = attention_forward(member_at, queries, key_rows, values_t)
        attended = group_all_to_all(outs)
        attended = (
            attended.reshape(splits, HEAD_GROUPS, query_rows, GROUP_COLS)
            .transpose(0, 2, 1, 3)
            .reshape(rows, D)
        )

        middle = resid + centered(dot(attended, w_out_all) + bias_out_all)
        inv_mlp = inverse_rms(middle)
        unit_mlp = middle * inv_mlp
        normed_mlp = (unit_mlp * gain_mlp_all).astype(bf16)
        grad_result = jnp.concatenate([grad_top, jnp.zeros((rows, 1), f32)], axis=1)
        grad_branch_mlp = centered(grad_result).astype(bf16)
        two_norm = jnp.concatenate([normed_mlp, to_core(normed_mlp)])
        two_grad = jnp.concatenate([grad_branch_mlp, to_core(grad_branch_mlp)])
        hidden = dot(two_norm, w_up_half) + bias_up_half
        active, gelu_back = jax.vjp(lambda h: jax.nn.gelu(h, approximate=True), hidden)
        active = active.astype(bf16)
        part_mlp = dot(active, w_down_half)
        grad_hidden = gelu_back(dot_nt(two_grad, w_down_half))[0].astype(bf16)
        part_norm = dot_nt(grad_hidden, w_up_half)
        part = jnp.stack([part_mlp, part_norm]).reshape(2, 2, rows, D)
        part_other = to_core(part[:, 1].astype(bf16))
        branch_mlp = part[0, 0] + part_other[0] + bias_down_all
        grad_norm = part[1, 0] + part_other[1]
        stream_out = (middle + centered(branch_mlp))[:, : D - 1].astype(bf16)
        grad_down = dot_tn(active, two_grad).astype(bf16)
        grad_up = dot_tn(two_norm, grad_hidden).astype(bf16)

        sum_gain_mlp = jnp.sum(grad_norm * unit_mlp, axis=0)
        scaled = grad_norm * gain_mlp_all
        grad_middle = grad_result + inv_mlp * (
            scaled - unit_mlp * jnp.mean(scaled * unit_mlp, axis=1, keepdims=True)
        )
        grad_branch = centered(grad_middle).astype(bf16)
        grad_out_w = dot_tn(attended, grad_branch).astype(bf16)
        grad_attended = dot_nt(grad_branch, w_out_all).astype(bf16)
        grad_attended = (
            grad_attended.reshape(splits, query_rows, HEAD_GROUPS, GROUP_COLS)
            .transpose(0, 2, 1, 3)
            .reshape(ctx_count, query_rows, GROUP_COLS)
        )
        grads = group_all_to_all(grad_attended)
        dq, dk, dv = attention_backward(
            member_at, queries, key_rows, values, keys_t, grads, outs, logs
        )

        grad_normed = dot_nt(dk.reshape(-1, GROUP_COLS), wk) + dot_nt(dv.reshape(-1, GROUP_COLS), wv)
        from_query = dot_nt(dq.reshape(-1, GROUP_COLS), wq).reshape(ctx_count, 1, query_rows, D)
        chosen = (jnp.arange(splits) == query_split)[None, :, None, None]
        grad_normed = grad_normed.reshape(ctx_count, splits, query_rows, D) + jnp.where(
            chosen, from_query, 0.0
        )
        grad_normed = grad_normed.reshape(ctx_count, rows, D).astype(bf16)
        both = grad_normed[:half] + to_core(grad_normed[half:])
        first, second = both[:, : rows // 2], both[:, rows // 2 :]
        second = jnp.stack([second[reversed_bits(slot)] for slot in range(half)])
        for step in reversed(range(steps)):
            keep = 1 << step
            got = (
                to_ctx(first[keep:], 1 << step),
                to_ctx(second[keep:], 1 << (steps - 1 - step)),
            )
            got = lax.optimization_barrier(got)
            first, second = first[:keep] + got[0], second[:keep] + got[1]
        grad_normed = jnp.concatenate([first[0], second[0]]).astype(f32)

        sum_gain_attn = jnp.sum(grad_normed * unit, axis=0)
        scaled = grad_normed * gain_attn_all
        grad_resid = grad_middle + inv_attn * (
            scaled - unit * jnp.mean(scaled * unit, axis=1, keepdims=True)
        )
        grad_stream = (grad_resid[:, : D - 1] - grad_resid[:, D - 1 :]).astype(bf16)

        def scatter_ctx(value, first_bit=0):
            for step in range(first_bit, ctx_steps):
                bit = (ctx_at >> step) & 1
                parts = value.reshape((value.shape[0] // 2, 2) + value.shape[1:])
                value = pick(parts, bit, 1) + to_ctx(pick(parts, 1 - bit, 1), 1 << step)
            return value[0]

        def gather_ctx(value, first_bit, last_bit):
            value = value[None]
            for step in reversed(range(first_bit, last_bit)):
                pair = in_order(value, to_ctx(value, 1 << step), (ctx_at >> step) & 1)
                value = jnp.swapaxes(pair, 0, 1).reshape((-1,) + value.shape[1:])
            return value

        down = grad_down.reshape(2, -1, D)
        down = pick(down, chip_row) + to_chip_row(pick(down, 1 - chip_row))
        down = scatter_ctx(down.reshape(ctx_count, -1, D))
        grad_w_down = gather_ctx(down, 0, ctx_steps).reshape(-1, D).astype(f32)

        up = grad_up.reshape(2, 2, shard, -1)
        up = pick(up, chip_row) + to_chip_row(pick(up, 1 - chip_row))
        up = scatter_ctx(
            up.reshape(2, ctx_count, shard // ctx_count, -1).transpose(1, 0, 2, 3)
        ).reshape(2, shard // ctx_count, 2, -1)
        up = in_order(pick(up, core), to_core(pick(up, 1 - core)), core)
        up = up.transpose(1, 2, 0, 3).reshape(shard // ctx_count, -1)
        grad_w_up = gather_ctx(up, 0, ctx_steps).reshape(shard, -1).astype(f32)

        def over_rows(value):
            value = value.reshape((2, 2, shard) + value.shape[1:])
            value = pick(value, core, 1) + to_core(pick(value, 1 - core, 1))
            return pick(value, chip_row) + to_chip_row(pick(value, 1 - chip_row))

        out_w = scatter_ctx(over_rows(grad_out_w).reshape(ctx_count, -1, D))
        grad_w_out = gather_ctx(out_w, 0, ctx_steps).reshape(shard, D).astype(f32)

        heads_w = jnp.concatenate(
            [
                dot_tn(normed_query.reshape(-1, D), dq.reshape(-1, GROUP_COLS)),
                dot_tn(flat, dk.reshape(-1, GROUP_COLS)),
                dot_tn(flat, dv.reshape(-1, GROUP_COLS)),
            ],
            axis=1,
        ).astype(bf16)
        heads_w = over_rows(heads_w).reshape(splits, -1, 3 * GROUP_COLS)
        heads_w = scatter_ctx(heads_w, 2)
        heads_w = gather_ctx(heads_w, 2, ctx_steps).reshape(shard, 3, GROUP_COLS)
        heads_w = gather_ctx(heads_w, 0, 2)
        grad_w_qkv = heads_w.transpose(1, 2, 0, 3).reshape(shard, 3 * D).astype(f32)

        def placed(value, parts, index):
            return jnp.where(
                (jnp.arange(parts) == index)[:, None], value.reshape(1, -1), 0.0
            ).reshape(-1)

        up_sum = jnp.sum(grad_hidden.astype(f32), axis=0).reshape(2, 1, -1)
        up_sum = jnp.where((jnp.arange(2) == core)[None, :, None], up_sum, 0.0).reshape(-1)
        sums = (
            sum_gain_attn,
            placed(jnp.sum(dq.astype(f32), axis=(0, 1)), HEAD_GROUPS, head_group),
            placed(jnp.sum(dv.astype(f32), axis=(0, 1)), HEAD_GROUPS, head_group),
            jnp.sum(grad_branch.astype(f32), axis=0),
            sum_gain_mlp,
            up_sum,
            jnp.sum(grad_branch_mlp.astype(f32), axis=0),
        )
        total = lax.psum(jnp.concatenate(sums), AXES)
        vector_outs, at = [], 0
        for width in (D, 2 * D, D, D, up_sum.shape[0], D):
            vector_outs.append(pick(total[at : at + width].reshape(fsdp_count, -1), fsdp_at))
            at += width
        v_gain_attn, v_bias_qv, v_bias_out, v_gain_mlp, v_bias_up, v_bias_down = vector_outs

        return (
            swap_sequences(stream_out),
            swap_sequences(grad_stream).astype(f32),
            v_gain_attn,
            grad_w_qkv,
            v_bias_qv,
            grad_w_out,
            v_bias_out,
            v_gain_mlp,
            grad_w_up,
            v_bias_up,
            grad_w_down,
            v_bias_down,
        )

    rows_spec, matrix_spec, vector_spec = P(AXES, None), P("fsdp", None), P("fsdp")
    return jax.shard_map(
        local,
        mesh=mesh,
        in_specs=(
            rows_spec,
            vector_spec,
            matrix_spec,
            vector_spec,
            matrix_spec,
            vector_spec,
            vector_spec,
            matrix_spec,
            vector_spec,
            matrix_spec,
            vector_spec,
            rows_spec,
        ),
        out_specs=(
            rows_spec,
            rows_spec,
            vector_spec,
            matrix_spec,
            vector_spec,
            matrix_spec,
            vector_spec,
            vector_spec,
            matrix_spec,
            vector_spec,
            matrix_spec,
            vector_spec,
        ),
        check_vma=False,
    )
```

time: 1070 us -> 498 us (0.47)
  the two profiles are of different devices: /device:TPU:0 before, /device:TPU:1 now
where the time goes in v1:
time: 498 us; the launch traced here: 488 us
  local copies, waits for them, and re-layouts  103 us (21%)
  waiting for transfers between devices  86.5 us (17%)
  other arithmetic  81.4 us (16%)
  starting transfers between devices  77.8 us (16%)
  Pallas kernels  55.5 us (11%)
  blocking collectives  41.6 us (8%)
  matrix products  39.6 us (8%)
    ppermute x55, waiting for transfers between devices, send(): return lax.ppermute(value, AXES, pairs)  86.5 us
    ppermute x55, starting transfers between devices, send(): return lax.ppermute(value, AXES, pairs)  66.2 us
    psum x1, blocking collectives, local(): total = lax.psum(jnp.concatenate(sums), AXES)  41.6 us
    select_n x22, other arithmetic, in_order(): return jnp.where(bit == 0, jnp.stack([own, other]), jnp.stack([other, own]))  35 us
    pallas_call x1, Pallas kernels, attention_backward(): pl.pallas_call(backward_kernel, out_shape=(jax.ShapeDtypeStruct((blocks,...  31.8 us
    pallas_call x1, Pallas kernels, attention_forward(): pl.pallas_call(forward_kernel, out_shape=(jax.ShapeDtypeStruct((blocks, q...  23.7 us
    select_n x5, local copies, waits for them, and re-layouts, in_order(): return jnp.where(bit == 0, jnp.stack([own, other]), jnp.stack([other, own]))  15 us
    dot_general x6, matrix products, dot_tn(): lax.dot_general(left, right, (((0,), (0,)), ((), ())), preferred_element_...  13 us
  transfers between devices with their start and end apart: 57, of which 18 were waited for; matrix products, arithmetic and copies ran while one was open for 41% of the time, Pallas kernels for 11%

profile of v1, /device:TPU:1, one launch (start us, length us, event | category | flops | bytes accessed | tf_op | source)
XLA Modules:
  0.0 488.4 jit_solution(3126941093279653216)
XLA Ops:
  0.7 4.2 concatenate.207
  7.0 5.5 %collective-permute-start = (bf16[256,767]{1,0:T(8,128)(2,1)}, bf16[256,767]{1,0:T(8,128)(2,1)}, u32[]{:S(2)}, u32[]{:S(2)}) collective-permute-start(bf16[256,767]{1,0:T(8,128)(2,1)} %param.12), channel_id=1, source_target_pairs={{0,0},{1,1},{2,2},{3,3},{4,8},{5,9},{6,10},{7,11},{8,4},{9,5},{10,... | collective-permute-start | bytes 1178120 | tf_op jit(solution)/shard_map/ppermute | solution.py:219
  12.5 2.9 reshape.966
  40.9 4.2 collective-permute-done.3
  48.0 3.0 collective-permute-start.5
  54.8 4.3 collective-permute-start.16
  92.2 23.7 %attend.1 = (bf16[8,128,192]{2,1,0:T(8,128)(2,1)S(1)}, f32[8,8,128]{2,1,0:T(8,128)S(1)}) custom-call(s32[1]{0:T(128)} %bitcast.1.member_ref, bf16[8,128,192]{2,1,0:T(8,128)(2,1)S(1)} %fusion.19.q_ref, bf16[8,256,192]{2,1,0:T(8,128)(2,1)S(1)} %convolution_convert_fusion.4.k_ref, bf16[192,2048]{1,0:T(8,128)(2,1)S(1)} %fusion.10.vt_ref), custom_call_target="tpu_custom_call" | custom-call | flops 905969664 | bytes 1572864 | tf_op jit(solution)/shard_map/attend/pallas_call | solution.py:110
  116.9 5.0 %all-to-all-start = ((bf16[8,128,192]{1,2,0:T(8,128)(2,1)}), bf16[8,128,192]{1,2,0:T(8,128)(2,1)}, u32[]{:S(2)}, u32[]{:S(2)}) async-start(bf16[8,128,192]{1,2,0:T(8,128)(2,1)} %copy.394), calls=%async_computation | async-start | bytes 786432 | tf_op jit(solution)/shard_map/all_to_all | solution.py:242
  125.4 3.9 maximum_select_fusion.1
  131.2 3.8 copy.401
  135.1 6.3 %reshape.1008 = bf16[768,1536,1]{1,0,2:T(8,128)(2,1)} reshape(bf16[2,2,192,2,768]{4,3,2,1,0:T(2,128)(2,1)} %copy.401) | data formatting | bytes 4718592 | tf_op jit(solution)/shard_map/jit(_where)/select_n | solution.py:42
  141.4 3.5 copy.454
  154.0 4.1 add_convert_fusion.v_ref
  158.1 3.1 multiply_convert_fusion.1
  161.3 5.1 %convert_reduce_fusion = (f32[1536]{0:T(1024)S(1)}, bf16[512,1536]{1,0:T(8,128)(2,1)S(1)}) fusion(f32[512,1536]{1,0:T(8,128)S(1)} %get-tuple-element.85, bf16[1536,768]{1,0:T(8,128)(2,1)S(1)} %bitcast.375, bf16[256,768]{1,0:T(8,128)(2,1)} %collective-permute-done.17, bf16[256,768]{1,0:T(8,128)(2,1)} %get-tuple-element.43), kind=kOutput, calls=%fused_computation.21 | convolution fusion | flops 1226832384 | bytes 7870464 | tf_op jit(solution)/shard_map/dot_general | solution.py:34
  172.6 4.4 convolution_convert_fusion.1
  194.0 6.6 %all-to-all-start.1 = ((bf16[8,128,192]{1,2,0:T(8,128)(2,1)}), bf16[8,128,192]{1,2,0:T(8,128)(2,1)}, u32[]{:S(2)}, u32[]{:S(2)}) async-start(bf16[8,128,192]{1,2,0:T(8,128)(2,1)} %bitcast.55), calls=%async_computation.1 | async-start | bytes 786432 | tf_op jit(solution)/shard_map/all_to_all | solution.py:242
  211.5 20.8 %collective-permute-done.48 = bf16[768,768]{1,0:T(8,128)(2,1)} collective-permute-done((bf16[768,768]{1,0:T(8,128)(2,1)}, bf16[768,768]{1,0:T(8,128)(2,1)}, u32[]{:S(2)}, u32[]{:S(2)}) %collective-permute-start.48) | collective-permute-done | bytes 1179680 | tf_op jit(solution)/shard_map/ppermute | solution.py:219
  239.8 31.8 %attend_back.1 = (bf16[8,128,192]{2,1,0:T(8,128)(2,1)S(1)}, bf16[8,256,192]{2,1,0:T(8,128)(2,1)S(1)}, bf16[8,256,192]{2,1,0:T(8,128)(2,1)}) custom-call(s32[1]{0:T(128)} %bitcast.1.member_ref, bf16[8,128,192]{2,1,0:T(8,128)(2,1)S(1)} %fusion.19.q_ref, bf16[8,256,192]{2,1,0:T(8,128)(2,1)} %copy-done, bf16[8,256,192]{2,1,0:T(8,128)(2,1)} %add_convert_fusion.v_ref, ...), custom_call_target="tpu_custom_call" | custom-call | flops 2264924160 | bytes 3932160 | tf_op jit(solution)/shard_map/attend_back/pallas_call | solution.py:183
  300.2 4.2 collective-permute-done.35
  304.7 5.9 %collective-permute-done.36 = bf16[1,24,768]{2,1,0:T(8,128)(2,1)S(1)} collective-permute-done((bf16[1,24,768]{2,1,0:T(8,128)(2,1)S(1)}, bf16[1,24,768]{2,1,0:T(8,128)(2,1)S(1)}, u32[]{:S(2)}, u32[]{:S(2)}) %collective-permute-start.36) | collective-permute-done | bytes 36896 | tf_op jit(solution)/shard_map/ppermute | solution.py:219
  310.6 2.8 collective-permute-start.37
  315.2 3.5 collective-permute-done.38
  326.8 7.7 %collective-permute-done.43 = bf16[1,2,24,1536]{3,2,1,0:T(8,128)(2,1)S(1)} collective-permute-done((bf16[1,2,24,1536]{3,2,1,0:T(8,128)(2,1)S(1)}, bf16[1,2,24,1536]{3,2,1,0:T(8,128)(2,1)S(1)}, u32[]{:S(2)}, u32[]{:S(2)}) %collective-permute-start.43) | collective-permute-done | bytes 147488 | tf_op jit(solution)/shard_map/ppermute | solution.py:219
  337.8 3.0 collective-permute-start.44
  348.4 12.5 %collective-permute-done.29 = bf16[1,96,576]{2,1,0:T(8,128)(2,1)} collective-permute-done((bf16[1,96,576]{2,1,0:T(8,128)(2,1)}, bf16[1,96,576]{2,1,0:T(8,128)(2,1)}, u32[]{:S(2)}, u32[]{:S(2)}) %collective-permute-start.29) | collective-permute-done | bytes 110624 | tf_op jit(solution)/shard_map/ppermute | solution.py:219
  400.8 3.2 copy.423
  404.0 2.8 reshape.1000
  415.5 8.5 %collective-permute-done.47 = bf16[4,24,3072]{2,1,0:T(8,128)(2,1)} collective-permute-done((bf16[4,24,3072]{2,1,0:T(8,128)(2,1)S(1)}, bf16[4,24,3072]{2,1,0:T(8,128)(2,1)}, u32[]{:S(2)}, u32[]{:S(2)}) %collective-permute-start.47) | collective-permute-done | bytes 589856 | tf_op jit(solution)/shard_map/ppermute | solution.py:219
  428.8 41.6 %psum.7 = f32[7680]{0:T(1024)S(1)} all-reduce(f32[7680]{0:T(1024)S(1)} %constant_dynamic-update-slice_fusion), channel_id=1, replica_groups=mesh['fsdp'=4,'ctx'=8] {'fsdp','ctx'}, use_global_device_ids=true, to_apply=%region_16.17 | all-reduce | flops 7680 | bytes 61440 | tf_op jit(solution)/shard_map/psum | solution.py:468
  471.0 3.6 collective-permute-start.25
  478.5 6.8 %collective-permute-done.25 = bf16[256,767]{1,0:T(8,128)(2,1)S(1)} collective-permute-done((bf16[256,767]{1,0:T(8,128)(2,1)S(1)}, bf16[256,767]{1,0:T(8,128)(2,1)S(1)}, u32[]{:S(2)}, u32[]{:S(2)}) %collective-permute-start.25) | collective-permute-done | bytes 392736 | tf_op jit(solution)/shard_map/ppermute | solution.py:219
  (472 shorter events, 233.3 us)
Async XLA Ops:
  4.9 20.5 %collective-permute-start.6 = (bf16[1920]{0:T(1024)(128)(2,1)S(1)}, bf16[1920]{0:T(1024)(128)(2,1)S(1)}, u32[]{:S(2)}, u32[]{:S(2)}) collective-permute-start(bf16[1920]{0:T(1024)(128)(2,1)S(1)} %concatenate.207), channel_id=1, source_target_pairs={{0,16},{1,17},{2,18},{3,19},{4,20},{5,21},{6,22},{7,23},{8,24},{9,... | collective-permute-start | bytes 11528 | tf_op jit(solution)/shard_map/ppermute | solution.py:219
  6.9 62.5 %collective-permute-start.10 = (bf16[192,768]{1,0:T(8,128)(2,1)}, bf16[192,768]{1,0:T(8,128)(2,1)}, u32[]{:S(2)}, u32[]{:S(2)}) collective-permute-start(bf16[192,768]{1,0:T(8,128)(2,1)} %param.16), channel_id=1, source_target_pairs={{0,16},{1,17},{2,18},{3,19},{4,20},{5,21},{6,22},{7,23},{8,24},{9,... | collective-permute-start | bytes 884744 | tf_op jit(solution)/shard_map/ppermute | solution.py:219
  7.0 18.4 %collective-permute-start = (bf16[256,767]{1,0:T(8,128)(2,1)}, bf16[256,767]{1,0:T(8,128)(2,1)}, u32[]{:S(2)}, u32[]{:S(2)}) collective-permute-start(bf16[256,767]{1,0:T(8,128)(2,1)} %param.12), channel_id=1, source_target_pairs={{0,0},{1,1},{2,2},{3,3},{4,8},{5,9},{6,10},{7,11},{8,4},{9,5},{10,... | collective-permute-start | bytes 1178120 | tf_op jit(solution)/shard_map/ppermute | solution.py:219
  17.5 37.3 %collective-permute-start.8 = (bf16[192,576]{0,1:T(8,128)(2,1)}, bf16[192,576]{0,1:T(8,128)(2,1)}, u32[]{:S(2)}, u32[]{:S(2)}) collective-permute-start(bf16[192,576]{0,1:T(8,128)(2,1)} %bitcast.10), channel_id=1, source_target_pairs={{0,16},{1,17},{2,18},{3,19},{4,20},{5,21},{6,22},{7,23},{8,24},{9,... | collective-permute-start | bytes 663560 | tf_op jit(solution)/shard_map/ppermute | solution.py:219
  37.8 37.3 %collective-permute-start.13 = (bf16[192,2,768]{2,0,1:T(8,128)(2,1)}, bf16[192,2,768]{2,0,1:T(8,128)(2,1)}, u32[]{:S(2)}, u32[]{:S(2)}) collective-permute-start(bf16[192,2,768]{2,0,1:T(8,128)(2,1)} %bitcast.339), channel_id=1, source_target_pairs={{0,8},{1,9},{2,10},{3,11},{4,12},{5,13},{6,14},{7,15},{8,0},{9,1},... | collective-permute-start | bytes 1769480 | tf_op jit(solution)/shard_map/ppermute | solution.py:219
  45.0 80.3 %collective-permute-start.15 = (bf16[768,768]{1,0:T(8,128)(2,1)}, bf16[768,768]{1,0:T(8,128)(2,1)}, u32[]{:S(2)}, u32[]{:S(2)}) collective-permute-start(bf16[768,768]{1,0:T(8,128)(2,1)} %param.21), channel_id=1, source_target_pairs={{0,16},{1,17},{2,18},{3,19},{4,20},{5,21},{6,22},{7,23},{8,24},{9,... | collective-permute-start | bytes 3538952 | tf_op jit(solution)/shard_map/ppermute | solution.py:219
  48.0 36.0 %collective-permute-start.5 = (bf16[4,256,768]{2,1,0:T(8,128)(2,1)}, bf16[4,256,768]{2,1,0:T(8,128)(2,1)S(1)}, u32[]{:S(2)}, u32[]{:S(2)}) collective-permute-start(bf16[4,256,768]{2,1,0:T(8,128)(2,1)} %maximum_maximum_fusion), channel_id=1, source_target_pairs={{0,8},{1,9},{2,10},{3,11},{4,12},{5,13},{6,14},{7,15},{8,0},{9,1},... | collective-permute-start | bytes 4718600 | tf_op jit(solution)/shard_map/ppermute | solution.py:219
  54.8 18.9 %collective-permute-start.16 = (bf16[256,767]{1,0:T(8,128)(2,1)}, bf16[256,767]{1,0:T(8,128)(2,1)S(1)}, u32[]{:S(2)}, u32[]{:S(2)}) collective-permute-start(bf16[256,767]{1,0:T(8,128)(2,1)} %param.23), channel_id=1, source_target_pairs={{0,0},{1,1},{2,2},{3,3},{4,8},{5,9},{6,10},{7,11},{8,4},{9,5},{10,... | collective-permute-start | bytes 1178120 | tf_op jit(solution)/shard_map/ppermute | solution.py:219
  73.6 49.8 %collective-permute-start.11 = (bf16[2,192,768]{2,1,0:T(8,128)(2,1)}, bf16[2,192,768]{2,1,0:T(8,128)(2,1)}, u32[]{:S(2)}, u32[]{:S(2)}) collective-permute-start(bf16[2,192,768]{2,1,0:T(8,128)(2,1)} %maximum_select_fusion.11), channel_id=1, source_target_pairs={{0,8},{1,9},{2,10},{3,11},{4,12},{5,13},{6,14},{7,15},{8,0},{9,1},... | collective-permute-start | bytes 1769480 | tf_op jit(solution)/shard_map/ppermute | solution.py:219
  75.2 86.1 %collective-permute-start.17 = (bf16[256,768]{1,0:T(8,128)(2,1)}, bf16[256,768]{1,0:T(8,128)(2,1)}, u32[]{:S(2)}, u32[]{:S(2)}) collective-permute-start(bf16[256,768]{1,0:T(8,128)(2,1)} %get-tuple-element.43), channel_id=1, source_target_pairs={{0,8},{1,9},{2,10},{3,11},{4,12},{5,13},{6,14},{7,15},{8,0},{9,1},... | collective-permute-start | bytes 1179656 | tf_op jit(solution)/shard_map/ppermute | solution.py:219
  77.7 51.6 %collective-permute-start.14 = (bf16[2,192,2,768]{3,1,2,0:T(8,128)(2,1)}, bf16[2,192,2,768]{3,1,2,0:T(8,128)(2,1)}, u32[]{:S(2)}, u32[]{:S(2)}) collective-permute-start(bf16[2,192,2,768]{3,1,2,0:T(8,128)(2,1)} %maximum_select_fusion.5), channel_id=1, source_target_pairs={{0,16},{1,17},{2,18},{3,19},{4,20},{5,21},{6,22},{7,23},{8,24},{9,... | collective-permute-start | bytes 3538952 | tf_op jit(solution)/shard_map/ppermute | solution.py:219
  116.9 28.0 %all-to-all-start = ((bf16[8,128,192]{1,2,0:T(8,128)(2,1)}), bf16[8,128,192]{1,2,0:T(8,128)(2,1)}, u32[]{:S(2)}, u32[]{:S(2)}) async-start(bf16[8,128,192]{1,2,0:T(8,128)(2,1)} %copy.394), calls=%async_computation | async-start | bytes 786432 | tf_op jit(solution)/shard_map/all_to_all | solution.py:242
  179.6 27.4 %collective-permute-start.40 = (bf16[2,192,1536]{2,1,0:T(8,128)(2,1)}, bf16[2,192,1536]{2,1,0:T(8,128)(2,1)}, u32[]{:S(2)}, u32[]{:S(2)}) collective-permute-start(bf16[2,192,1536]{2,1,0:T(8,128)(2,1)} %dynamic-slice_bitcast_fusion.1), channel_id=1, source_target_pairs={{0,16},{1,17},{2,18},{3,19},{4,20},{5,21},{6,22},{7,23},{8,24},{9,... | collective-permute-start | bytes 3538952 | tf_op jit(solution)/shard_map/ppermute | solution.py:219
  184.2 48.1 %collective-permute-start.48 = (bf16[768,768]{1,0:T(8,128)(2,1)}, bf16[768,768]{1,0:T(8,128)(2,1)}, u32[]{:S(2)}, u32[]{:S(2)}) collective-permute-start(bf16[768,768]{1,0:T(8,128)(2,1)} %dynamic-slice_bitcast_fusion), channel_id=1, source_target_pairs={{0,16},{1,17},{2,18},{3,19},{4,20},{5,21},{6,22},{7,23},{8,24},{9,... | collective-permute-start | bytes 3538952 | tf_op jit(solution)/shard_map/ppermute | solution.py:219
  194.0 44.5 %all-to-all-start.1 = ((bf16[8,128,192]{1,2,0:T(8,128)(2,1)}), bf16[8,128,192]{1,2,0:T(8,128)(2,1)}, u32[]{:S(2)}, u32[]{:S(2)}) async-start(bf16[8,128,192]{1,2,0:T(8,128)(2,1)} %bitcast.55), calls=%async_computation.1 | async-start | bytes 786432 | tf_op jit(solution)/shard_map/all_to_all | solution.py:242
  202.3 34.4 %collective-permute-start.32 = (bf16[2,192,768]{2,1,0:T(8,128)(2,1)S(1)}, bf16[2,192,768]{2,1,0:T(8,128)(2,1)S(1)}, u32[]{:S(2)}, u32[]{:S(2)}) collective-permute-start(bf16[2,192,768]{2,1,0:T(8,128)(2,1)S(1)} %dynamic-slice_bitcast_fusion.4), channel_id=1, source_target_pairs={{0,8},{1,9},{2,10},{3,11},{4,12},{5,13},{6,14},{7,15},{8,0},{9,1},... | collective-permute-start | bytes 1769480 | tf_op jit(solution)/shard_map/ppermute | solution.py:219
  209.5 83.7 %collective-permute-start.41 = (bf16[4,2,24,1536]{3,2,1,0:T(8,128)(2,1)}, bf16[4,2,24,1536]{3,2,1,0:T(8,128)(2,1)}, u32[]{:S(2)}, u32[]{:S(2)}) collective-permute-start(bf16[4,2,24,1536]{3,2,1,0:T(8,128)(2,1)} %dynamic-slice_bitcast_fusion.3), channel_id=1, source_target_pairs={{0,1},{1,0},{2,3},{3,2},{4,5},{5,4},{6,7},{7,6},{8,9},{9,8},{10,11... | collective-permute-start | bytes 1769480 | tf_op jit(solution)/shard_map/ppermute | solution.py:219
  234.7 61.2 %collective-permute-start.49 = (bf16[4,96,768]{2,1,0:T(8,128)(2,1)}, bf16[4,96,768]{2,1,0:T(8,128)(2,1)}, u32[]{:S(2)}, u32[]{:S(2)}) collective-permute-start(bf16[4,96,768]{2,1,0:T(8,128)(2,1)} %dynamic-slice_bitcast_fusion.2), channel_id=1, source_target_pairs={{0,1},{1,0},{2,3},{3,2},{4,5},{5,4},{6,7},{7,6},{8,9},{9,8},{10,11... | collective-permute-start | bytes 1769480 | tf_op jit(solution)/shard_map/ppermute | solution.py:219
  237.6 54.5 %collective-permute-start.33 = (bf16[192,768]{1,0:T(8,128)(2,1)}, bf16[192,768]{1,0:T(8,128)(2,1)}, u32[]{:S(2)}, u32[]{:S(2)}) collective-permute-start(bf16[192,768]{1,0:T(8,128)(2,1)} %dynamic-slice_bitcast_fusion.8), channel_id=1, source_target_pairs={{0,16},{1,17},{2,18},{3,19},{4,20},{5,21},{6,22},{7,23},{8,24},{9,... | collective-permute-start | bytes 884744 | tf_op jit(solution)/shard_map/ppermute | solution.py:219
  281.5 105.2 %collective-permute-start.20 = (bf16[4,256,768]{2,1,0:T(8,128)(2,1)}, bf16[4,256,768]{2,1,0:T(8,128)(2,1)}, u32[]{:S(2)}, u32[]{:S(2)}) collective-permute-start(bf16[4,256,768]{2,1,0:T(8,128)(2,1)} %slice.255), channel_id=1, source_target_pairs={{0,8},{1,9},{2,10},{3,11},{4,12},{5,13},{6,14},{7,15},{8,0},{9,1},... | collective-permute-start | bytes 4718600 | tf_op jit(solution)/shard_map/ppermute | solution.py:219
  294.4 25.6 %collective-permute-start.42 = (bf16[2,2,24,1536]{3,2,1,0:T(8,128)(2,1)S(1)}, bf16[2,2,24,1536]{3,2,1,0:T(8,128)(2,1)S(1)}, u32[]{:S(2)}, u32[]{:S(2)}) collective-permute-start(bf16[2,2,24,1536]{3,2,1,0:T(8,128)(2,1)S(1)} %dynamic-slice_bitcast_fusion.7), channel_id=1, source_target_pairs={{0,2},{1,3},{2,0},{3,1},{4,6},{5,7},{6,4},{7,5},{8,10},{9,11},{10,... | collective-permute-start | bytes 884744 | tf_op jit(solution)/shard_map/ppermute | solution.py:219
  299.8 22.2 %collective-permute-start.50 = (bf16[2,96,768]{2,1,0:T(8,128)(2,1)S(1)}, bf16[2,96,768]{2,1,0:T(8,128)(2,1)S(1)}, u32[]{:S(2)}, u32[]{:S(2)}) collective-permute-start(bf16[2,96,768]{2,1,0:T(8,128)(2,1)S(1)} %dynamic-slice_bitcast_fusion.6), channel_id=1, source_target_pairs={{0,2},{1,3},{2,0},{3,1},{4,6},{5,7},{6,4},{7,5},{8,10},{9,11},{10,... | collective-permute-start | bytes 884744 | tf_op jit(solution)/shard_map/ppermute | solution.py:219
  322.9 18.0 %collective-permute-start.51 = (bf16[1,96,768]{2,1,0:T(8,128)(2,1)}, bf16[1,96,768]{2,1,0:T(8,128)(2,1)}, u32[]{:S(2)}, u32[]{:S(2)}) collective-permute-start(bf16[1,96,768]{2,1,0:T(8,128)(2,1)} %constant_dynamic-slice_fusion.2), channel_id=1, source_target_pairs={{0,4},{1,5},{2,6},{3,7},{4,0},{5,1},{6,2},{7,3},{8,12},{9,13},{10,... | collective-permute-start | bytes 442376 | tf_op jit(solution)/shard_map/ppermute | solution.py:219
  324.0 18.6 %collective-permute-start.28 = (bf16[1,96,576]{2,1,0:T(8,128)(2,1)}, bf16[1,96,576]{2,1,0:T(8,128)(2,1)}, u32[]{:S(2)}, u32[]{:S(2)}) collective-permute-start(bf16[1,96,576]{2,1,0:T(8,128)(2,1)} %dynamic-slice_bitcast_fusion.11), channel_id=1, source_target_pairs={{0,4},{1,5},{2,6},{3,7},{4,0},{5,1},{6,2},{7,3},{8,12},{9,13},{10,... | collective-permute-start | bytes 331784 | tf_op jit(solution)/shard_map/ppermute | solution.py:219
  342.6 24.2 %collective-permute-start.52 = (bf16[1,96,768]{2,1,0:T(8,128)(2,1)}, bf16[1,96,768]{2,1,0:T(8,128)(2,1)}, u32[]{:S(2)}, u32[]{:S(2)}) collective-permute-start(bf16[1,96,768]{2,1,0:T(8,128)(2,1)} %dynamic-slice_add_fusion), channel_id=1, source_target_pairs={{0,4},{1,5},{2,6},{3,7},{4,0},{5,1},{6,2},{7,3},{8,12},{9,13},{10,... | collective-permute-start | bytes 442376 | tf_op jit(solution)/shard_map/ppermute | solution.py:219
  348.4 23.6 %collective-permute-start.45 = (bf16[1,24,3072]{2,1,0:T(8,128)(2,1)}, bf16[1,24,3072]{2,1,0:T(8,128)(2,1)}, u32[]{:S(2)}, u32[]{:S(2)}) collective-permute-start(bf16[1,24,3072]{2,1,0:T(8,128)(2,1)} %broadcast_in_dim_reshape.2), channel_id=1, source_target_pairs={{0,4},{1,5},{2,6},{3,7},{4,0},{5,1},{6,2},{7,3},{8,12},{9,13},{10,... | collective-permute-start | bytes 442376 | tf_op jit(solution)/shard_map/ppermute | solution.py:219
  374.0 17.4 %collective-permute-start.46 = (bf16[2,24,3072]{2,1,0:T(8,128)(2,1)}, bf16[2,24,3072]{2,1,0:T(8,128)(2,1)}, u32[]{:S(2)}, u32[]{:S(2)}) collective-permute-start(bf16[2,24,3072]{2,1,0:T(8,128)(2,1)} %maximum_select_fusion.18), channel_id=1, source_target_pairs={{0,2},{1,3},{2,0},{3,1},{4,6},{5,7},{6,4},{7,5},{8,10},{9,11},{10,... | collective-permute-start | bytes 884744 | tf_op jit(solution)/shard_map/ppermute | solution.py:219
  376.8 17.3 %collective-permute-start.31 = (bf16[2,192,3,192]{1,3,2,0:T(8,128)(2,1)}, bf16[2,192,3,192]{1,3,2,0:T(8,128)(2,1)}, u32[]{:S(2)}, u32[]{:S(2)}) collective-permute-start(bf16[2,192,3,192]{1,3,2,0:T(8,128)(2,1)} %maximum_select_fusion.13), channel_id=1, source_target_pairs={{0,1},{1,0},{2,3},{3,2},{4,5},{5,4},{6,7},{7,6},{8,9},{9,8},{10,11... | collective-permute-start | bytes 1327112 | tf_op jit(solution)/shard_map/ppermute | solution.py:219
  385.2 21.5 %collective-permute-start.54 = (bf16[4,96,768]{2,1,0:T(8,128)(2,1)}, bf16[4,96,768]{2,1,0:T(8,128)(2,1)}, u32[]{:S(2)}, u32[]{:S(2)}) collective-permute-start(bf16[4,96,768]{2,1,0:T(8,128)(2,1)} %bitcast.150), channel_id=1, source_target_pairs={{0,1},{1,0},{2,3},{3,2},{4,5},{5,4},{6,7},{7,6},{8,9},{9,8},{10,11... | collective-permute-start | bytes 1769480 | tf_op jit(solution)/shard_map/ppermute | solution.py:219
  389.1 21.1 %collective-permute-start.21 = (bf16[2,128,768]{2,1,0:T(8,128)(2,1)}, bf16[2,128,768]{2,1,0:T(8,128)(2,1)}, u32[]{:S(2)}, u32[]{:S(2)}) collective-permute-start(bf16[2,128,768]{2,1,0:T(8,128)(2,1)} %slice.257), channel_id=1, source_target_pairs={{0,2},{1,3},{2,0},{3,1},{4,6},{5,7},{6,4},{7,5},{8,10},{9,11},{10,... | collective-permute-start | bytes 1179656 | tf_op jit(solution)/shard_map/ppermute | solution.py:219
  391.3 20.1 %collective-permute-start.22 = (bf16[2,128,768]{2,1,0:T(8,128)(2,1)}, bf16[2,128,768]{2,1,0:T(8,128)(2,1)}, u32[]{:S(2)}, u32[]{:S(2)}) collective-permute-start(bf16[2,128,768]{2,1,0:T(8,128)(2,1)} %pad_maximum_fusion.14), channel_id=1, source_target_pairs={{0,1},{1,0},{2,3},{3,2},{4,5},{5,4},{6,7},{7,6},{8,9},{9,8},{10,11... | collective-permute-start | bytes 1179656 | tf_op jit(solution)/shard_map/ppermute | solution.py:219
  392.6 31.5 %collective-permute-start.47 = (bf16[4,24,3072]{2,1,0:T(8,128)(2,1)S(1)}, bf16[4,24,3072]{2,1,0:T(8,128)(2,1)}, u32[]{:S(2)}, u32[]{:S(2)}) collective-permute-start(bf16[4,24,3072]{2,1,0:T(8,128)(2,1)S(1)} %bitcast.383), channel_id=1, source_target_pairs={{0,1},{1,0},{2,3},{3,2},{4,5},{5,4},{6,7},{7,6},{8,9},{9,8},{10,11... | collective-permute-start | bytes 1769480 | tf_op jit(solution)/shard_map/ppermute | solution.py:219
  (102 other events, 893.8 us)
